TPU v7x, 32 devices: a whole 2x2x4 slice. The times are simulated.
32 devices in a mesh: tm: 2 (over core), lat: 16 (over z, y, x).
Axes of the slice: x: 2, y: 2, z: 4, core: 2. Of those that a mesh axis runs over, the one named last changes fastest.
Arguments:
- spectral_state: float32 [4, 16, 2, 16, 256], P('tm', 'lat'), may hold values from -6 to 6
- legendre: bfloat16 [16, 16, 16], P('lat'), may hold values from -1.5 to 1.5
- wave_slots: int32 [16], replicated, may hold values from 0 to 15, each once
- lat_order: int32 [16], replicated, may hold values from 0 to 15, each once
- quad_weights: float32 [16], replicated, may hold values from 0.2 to 1
- available: int32 [4, 8, 16, 256], P('tm', None, 'lat'), may hold values 0 or 1
- targets: float32 [4, 4, 8], P('tm'), may hold values from -6 to 6
- w_first: float32 [256, 384], replicated, may hold values from -0.375 to 0.375
- w_mid: float32 [384, 384], replicated, may hold values from -0.3125 to 0.3125
- w_last: float32 [384, 256], replicated, may hold values from -0.3125 to 0.3125
- norm_bias: float32 [2, 1024], replicated, may hold values from -0.3 to 0.3
- mean_first: float32 [256, 384], replicated, may hold values from -0.00061035156 to 0.00061035156
- mean_mid: float32 [384, 384], replicated, may hold values from -0.00061035156 to 0.00061035156
- mean_last: float32 [384, 256], replicated, may hold values from -0.00061035156 to 0.00061035156
- mean_bias: float32 [2, 1024], replicated, may hold values from -0.00061035156 to 0.00061035156
- square_first: float32 [256, 384], replicated, may hold values from 3e-10 to 3e-08
- square_mid: float32 [384, 384], replicated, may hold values from 3e-10 to 3e-08
- square_last: float32 [384, 256], replicated, may hold values from 3e-10 to 3e-08
- square_bias: float32 [2, 1024], replicated, may hold values from 3e-10 to 3e-08
Outputs:
- loss: float32 [], replicated
- grad_norm: float32 [], replicated
- master_first: float32 [256, 384], replicated
- master_mid: float32 [384, 384], replicated
- master_last: float32 [384, 256], replicated
- master_bias: float32 [2, 1024], replicated
- new_mean_first: float32 [256, 384], replicated
- new_mean_mid: float32 [384, 384], replicated
- new_mean_last: float32 [384, 256], replicated
- new_mean_bias: float32 [2, 1024], replicated
- new_square_first: float32 [256, 384], replicated
- new_square_mid: float32 [384, 384], replicated
- new_square_last: float32 [384, 256], replicated
- new_square_bias: float32 [2, 1024], replicated
- half_first: bfloat16 [256, 384], replicated
- half_mid: bfloat16 [384, 384], replicated
- half_last: bfloat16 [384, 256], replicated
- half_bias: bfloat16 [2, 1024], replicated
Inputs may be any that keep to these rules, and one draw needn't show every extreme that they name: `wave_slots`: each wavenumber 0 to 15 stands in one slot; slot j lies on the device of index j // 1 of lat. `lat_order`: each latitude stands in one grid row.
All inputs are finite; a program needn't handle non-finite values. No bound on the sum of `available` on one device may be relied on, other than what follows from the above.
Results may differ from a plain program's by a relative error of at most 0.0082.
Values may be sent and summed in bfloat16 or wider, within the bound.
No kernel may reach another device: no remote copies, remote signals or barrier semaphores. Data moves between devices by JAX's collectives and lax.ppermute only.
A program may use at most 128 MiB of HBM per device.

v0:
```python
from functools import partial
import math
import jax
import jax.numpy as jnp
from jax import lax
from jax.sharding import PartitionSpec as P

STEPS = 4
EPS_NORM = 1e-05
STEP_SCALE = 0.5
CLIP_NORM = 1.0
LEARN_RATE = 0.01
BETA_ONE = 0.9
BETA_TWO = 0.95
EPS_ADAM = 1e-08
DECAY = 0.1
HIGH = lax.Precision.HIGHEST


def wave_tables(wave_slots, lon_count):
    product = wave_slots[:, None] * jnp.arange(lon_count, dtype=jnp.int32)[None, :] % lon_count
    phase = product.astype(jnp.float32) * (2.0 * math.pi / lon_count)
    inverse = jnp.stack([jnp.cos(phase), -jnp.sin(phase)], axis=1)
    scale = jnp.where(wave_slots == 0, 1.0, 2.0).astype(jnp.float32) / lon_count
    return (inverse.astype(jnp.bfloat16), (inverse * scale[:, None, None]).astype(jnp.bfloat16))


def layer_spans(chans, hidden):
    gains = [(0, chans), (chans, hidden), (chans + hidden, hidden)]
    biases = [(0, hidden), (hidden, hidden), (2 * hidden, chans)]
    return list(zip(gains, biases))


def norm_gain(x, gain):
    centre = x - jnp.mean(x, axis=-1, keepdims=True)
    return centre * lax.rsqrt(jnp.mean(centre * centre, axis=-1, keepdims=True) + EPS_NORM) * gain


def corrector_forward(x, weights, norm_bias):
    spans = layer_spans(weights[0].shape[0], weights[0].shape[1])
    saved = []
    for k in range(3):
        (gstart, gwidth), (bstart, bwidth) = spans[k]
        h_low = norm_gain(x, 1.0 + norm_bias[0, gstart : gstart + gwidth]).astype(jnp.bfloat16)
        z_val = (
            jnp.dot(h_low, weights[k], preferred_element_type=jnp.float32)
            + norm_bias[1, bstart : bstart + bwidth]
        )
        saved.append((x, h_low, z_val))
        x = jax.nn.gelu(z_val, approximate=False) if k < 2 else z_val
    return (x, saved)


def corrector_backward(grad, saved, weights, norm_bias):
    spans = layer_spans(weights[0].shape[0], weights[0].shape[1])
    weight_grads = [None, None, None]
    gain_parts = [None, None, None]
    bias_parts = [None, None, None]
    for k in (2, 1, 0):
        (gstart, gwidth), (bstart, bwidth) = spans[k]
        x, h_low, z_val = saved[k]
        if k < 2:
            grad = jax.vjp(partial(jax.nn.gelu, approximate=False), z_val)[1](grad)[0]
        grad_low = grad.astype(jnp.bfloat16)
        weight_grads[k] = lax.dot_general(
            h_low, grad_low, (((0,), (0,)), ((), ())), preferred_element_type=jnp.float32
        )
        bias_parts[k] = jnp.sum(grad_low, axis=0, dtype=jnp.float32)
        back_h = lax.dot_general(
            grad_low, weights[k], (((1,), (1,)), ((), ())), preferred_element_type=jnp.float32
        )
        grad, gain_parts[k] = jax.vjp(norm_gain, x, 1.0 + norm_bias[0, gstart : gstart + gwidth])[
            1
        ](back_h)
    vector_grad = jnp.stack([jnp.concatenate(gain_parts), jnp.concatenate(bias_parts)])
    return (grad, (weight_grads[0], weight_grads[1], weight_grads[2], vector_grad))


def adamw(weight, mean, square, grad):
    mean_new = BETA_ONE * mean + (1.0 - BETA_ONE) * grad
    square_new = BETA_TWO * square + (1.0 - BETA_TWO) * grad * grad
    weight_new = weight - LEARN_RATE * (
        mean_new / (jnp.sqrt(square_new) + EPS_ADAM) + DECAY * weight
    )
    return (weight_new, mean_new, square_new)


def per_device(
    spectral_state,
    legendre,
    wave_slots,
    lat_order,
    quad_weights,
    available,
    targets,
    w_first,
    w_mid,
    w_last,
    norm_bias,
    mean_first,
    mean_mid,
    mean_last,
    mean_bias,
    square_first,
    square_mid,
    square_last,
    square_bias,
):
    tdev, wdev, _, degrees, chans = spectral_state.shape
    fields = available.shape[1]
    rows_dev = available.shape[2]
    lon_count = available.shape[3]
    levels = chans // fields
    lat_index = lax.axis_index("lat")
    slots = lax.dynamic_slice_in_dim(wave_slots, lat_index * wdev, wdev)
    finv, ffw = wave_tables(wave_slots, lon_count)
    keep = (jnp.arange(degrees, dtype=jnp.int32)[None, :] >= slots[:, None]).astype(jnp.bfloat16)
    plg = jnp.take(legendre, lat_order, axis=2) * keep[:, :, None]
    qrow = jnp.take(quad_weights, lat_order)
    qlocal = lax.dynamic_slice_in_dim(qrow, lat_index * rows_dev, rows_dev)
    colw = qlocal[None, None, :, None] * available.astype(jnp.float32)
    den_part = jnp.sum(colw, axis=(2, 3))
    params = (w_first, w_mid, w_last, norm_bias)
    weights = (
        w_first.astype(jnp.bfloat16),
        w_mid.astype(jnp.bfloat16),
        w_last.astype(jnp.bfloat16),
    )

    def legendre_sum(piece):
        return jnp.einsum("mnr,tmprc->tmpnc", plg, piece, preferred_element_type=jnp.float32)

    def fourier_sum(table, piece):
        return jnp.einsum("mpk,tmprc->trkc", table, piece, preferred_element_type=jnp.float32)

    def to_grid(state):
        sums = jnp.einsum(
            "mnr,tmpnc->tmprc", plg, state.astype(jnp.bfloat16), preferred_element_type=jnp.float32
        ).astype(jnp.bfloat16)
        return fourier_sum(
            finv, lax.all_to_all(sums, "lat", split_axis=3, concat_axis=1, tiled=True)
        )

    def column_pass(grid):
        out, saved = corrector_forward(grid.reshape(-1, chans), weights, norm_bias)
        return (out.reshape(grid.shape), saved)

    states = []
    nums = []
    den_total = den_part
    state = spectral_state
    for s in range(STEPS):
        states.append(state)
        grid = to_grid(state)
        out, saved = column_pass(grid)
        pred = grid + STEP_SCALE * out
        num_part = jnp.einsum(
            "tfrk,trkfl->tf",
            colw,
            pred.reshape(tdev, rows_dev, lon_count, fields, levels),
            precision=HIGH,
        )
        num_total, den_total = lax.psum((num_part, den_part), "lat")
        nums.append(num_total)
        tend = (out * qlocal[None, :, None, None]).astype(jnp.bfloat16)
        coeff = jnp.einsum("mpk,trkc->tmprc", ffw, tend, preferred_element_type=jnp.float32).astype(
            jnp.bfloat16
        )
        spec = legendre_sum(lax.all_to_all(coeff, "lat", split_axis=1, concat_axis=3, tiled=True))
        state = state + STEP_SCALE * spec
    num_all = jnp.stack(nums)
    bias = num_all / (levels * den_total[None]) - jnp.moveaxis(targets, 1, 0)
    loss = lax.psum(jnp.sum(bias * bias) / STEPS, "tm")
    grad_bias = 2.0 * bias / (STEPS * levels * den_total[None])
    totals = tuple((jnp.zeros_like(p) for p in params))
    back_state = None
    for s in reversed(range(STEPS)):
        grid = to_grid(states[s])
        out, saved = column_pass(grid)
        scaled = jnp.moveaxis(colw * grad_bias[s][:, :, None, None], 1, 3)
        back_pred = jnp.broadcast_to(scaled[..., None], scaled.shape + (levels,)).reshape(
            grid.shape
        )
        back_out = STEP_SCALE * back_pred
        if back_state is not None:
            back_spec = (STEP_SCALE * back_state).astype(jnp.bfloat16)
            back_coeff = jnp.einsum(
                "mnr,tmpnc->tmprc", plg, back_spec, preferred_element_type=jnp.float32
            ).astype(jnp.bfloat16)
            back_tend = fourier_sum(
                ffw, lax.all_to_all(back_coeff, "lat", split_axis=3, concat_axis=1, tiled=True)
            )
            back_out = back_out + qlocal[None, :, None, None] * back_tend
        back_in, grads = corrector_backward(back_out.reshape(-1, chans), saved, weights, norm_bias)
        totals = tuple((a + b for a, b in zip(totals, grads)))
        if s > 0:
            back_grid = (back_pred + back_in.reshape(grid.shape)).astype(jnp.bfloat16)
            back_sums = jnp.einsum(
                "mpk,trkc->tmprc", finv, back_grid, preferred_element_type=jnp.float32
            ).astype(jnp.bfloat16)
            back_low = legendre_sum(
                lax.all_to_all(back_sums, "lat", split_axis=1, concat_axis=3, tiled=True)
            )
            back_state = back_low if back_state is None else back_state + back_low
    means = (mean_first, mean_mid, mean_last, mean_bias)
    squares = (square_first, square_mid, square_last, square_bias)
    grads = lax.psum(totals, ("tm", "lat"))
    grad_norm = jnp.sqrt(sum((jnp.sum(g * g) for g in grads)))
    factor = CLIP_NORM / jnp.maximum(grad_norm, CLIP_NORM)
    results = [adamw(w, a, b, g * factor) for w, a, b, g in zip(params, means, squares, grads)]
    masters = [r[0] for r in results]
    new_means = [r[1] for r in results]
    new_squares = [r[2] for r in results]
    halves = [w.astype(jnp.bfloat16) for w in masters]
    return (
        loss,
        grad_norm,
        masters[0],
        masters[1],
        masters[2],
        masters[3],
        new_means[0],
        new_means[1],
        new_means[2],
        new_means[3],
        new_squares[0],
        new_squares[1],
        new_squares[2],
        new_squares[3],
        halves[0],
        halves[1],
        halves[2],
        halves[3],
    )


def solution(mesh):
    in_specs = (
        P("tm", "lat", None, None, None),
        P("lat", None, None),
        P(),
        P(),
        P(),
        P("tm", None, "lat", None),
        P("tm", None, None),
        P(),
        P(),
        P(),
        P(),
        P(),
        P(),
        P(),
        P(),
        P(),
        P(),
        P(),
        P(),
    )
    out_specs = (
        P(),
        P(),
        P(),
        P(),
        P(),
        P(),
        P(),
        P(),
        P(),
        P(),
        P(),
        P(),
        P(),
        P(),
        P(),
        P(),
        P(),
        P(),
    )
    return jax.shard_map(
        per_device, mesh=mesh, in_specs=in_specs, out_specs=out_specs, check_vma=False
    )
```

profile of v0, /device:TPU:0, one launch (start us, length us, event | category | flops | bytes accessed | tf_op | source)
XLA Modules:
  0.0 490.8 jit_solution(849199737556524078)
XLA Ops:
  11.4 8.3 %all-to-all-start = ((bf16[2,1,2,16,256]{4,2,0,1,3:T(2,128)(2,1)}), bf16[2,1,2,16,256]{4,2,0,1,3:T(2,128)(2,1)S(1)}, u32[]{:S(2)}, u32[]{:S(2)}) async-start(bf16[2,1,2,16,256]{4,2,0,1,3:T(2,128)(2,1)} %copy.194), calls=%async_computation | async-start | bytes 65536 | tf_op jit(solution)/shard_map/all_to_all | solution.py:141
  21.9 5.3 %all-to-all-done = bf16[2,1,2,16,256]{4,2,0,1,3:T(2,128)(2,1)S(1)} async-done(((bf16[2,1,2,16,256]{4,2,0,1,3:T(2,128)(2,1)}), bf16[2,1,2,16,256]{4,2,0,1,3:T(2,128)(2,1)S(1)}, u32[]{:S(2)}, u32[]{:S(2)}) %all-to-all-start) | async-done | bytes 32800 | tf_op jit(solution)/shard_map/all_to_all | solution.py:141
  28.0 3.0 fusion.214
  31.9 3.2 fusion.212
  37.8 10.0 %all_to_all.215 = bf16[2,16,2,1,256]{4,2,0,3,1:T(2,128)(2,1)S(1)} all-to-all(bf16[2,16,2,1,256]{4,2,0,3,1:T(2,128)(2,1)S(1)} %copy.198), channel_id=1, replica_groups=mesh['tm'=2,'lat'=16] {'lat'}, dimensions={1} | all-to-all | bytes 65536 | tf_op jit(solution)/shard_map/all_to_all | solution.py:169
  48.2 10.1 %all_to_all.216 = bf16[2,1,2,16,256]{4,2,0,1,3:T(2,128)(2,1)S(1)} all-to-all(bf16[2,1,2,16,256]{4,2,0,1,3:T(2,128)(2,1)S(1)} %copy.202), channel_id=1, replica_groups=mesh['tm'=2,'lat'=16] {'lat'}, dimensions={3} | all-to-all | bytes 65536 | tf_op jit(solution)/shard_map/all_to_all | solution.py:141
  60.6 3.0 fusion.210
  64.5 3.2 fusion.208
  70.5 10.0 %all_to_all.217 = bf16[2,16,2,1,256]{4,2,0,3,1:T(2,128)(2,1)S(1)} all-to-all(bf16[2,16,2,1,256]{4,2,0,3,1:T(2,128)(2,1)S(1)} %copy.206), channel_id=1, replica_groups=mesh['tm'=2,'lat'=16] {'lat'}, dimensions={1} | all-to-all | bytes 65536 | tf_op jit(solution)/shard_map/all_to_all | solution.py:169
  80.8 10.0 %all_to_all.218 = bf16[2,1,2,16,256]{4,2,0,1,3:T(2,128)(2,1)S(1)} all-to-all(bf16[2,1,2,16,256]{4,2,0,1,3:T(2,128)(2,1)S(1)} %copy.209), channel_id=1, replica_groups=mesh['tm'=2,'lat'=16] {'lat'}, dimensions={3} | all-to-all | bytes 65536 | tf_op jit(solution)/shard_map/all_to_all | solution.py:141
  93.4 3.1 fusion.206
  96.7 3.2 fusion.204
  100.0 1.9 broadcast_multiply_fusion
  102.1 10.0 %all_to_all.219 = bf16[2,16,2,1,256]{4,2,0,3,1:T(2,128)(2,1)S(1)} all-to-all(bf16[2,16,2,1,256]{4,2,0,3,1:T(2,128)(2,1)S(1)} %copy.213), channel_id=1, replica_groups=mesh['tm'=2,'lat'=16] {'lat'}, dimensions={1} | all-to-all | bytes 65536 | tf_op jit(solution)/shard_map/all_to_all | solution.py:169
  113.0 3.8 all-to-all-start.6
  117.7 2.0 copy.197
  122.8 2.1 copy.205
  124.9 1.9 add.549
  127.9 2.1 copy.212
  130.0 1.9 add.558
  136.3 3.1 fusion.202
  140.6 3.2 fusion.200
  145.1 2.1 copy.219
  147.2 2.1 add.567
  150.4 42.5 %all-reduce.1 = (f32[1,2,8]{2,1,0:T(2,128)S(1)}, f32[1,2,8]{2,1,0:T(2,128)S(1)}, f32[1,2,8]{2,1,0:T(2,128)S(1)}, f32[1,2,8]{2,1,0:T(2,128)S(1)}, f32[2,8]{1,0:T(2,128)S(1)}) all-reduce(f32[1,2,8]{2,1,0:T(2,128)S(1)} %bitcast.673, f32[1,2,8]{2,1,0:T(2,128)S(1)} %bitcast.674, ...), channel_id=1, replica_groups=mesh['tm'=2,'lat'=16] {'lat'}, use_global_device_ids=true, to_apply=%region_31.32 | all-reduce | flops 80 | bytes 640 | tf_op jit(solution)/shard_map/psum | solution.py:163
  203.2 1.9 convert_reduce_fusion.7
  205.1 2.8 multiply_reduce_fusion.27
  208.6 2.2 fusion.220
  210.8 3.4 psum.75
  218.5 2.0 copy.233
  221.4 2.0 copy.253
  224.2 2.0 copy.243
  230.8 3.6 all-to-all-start.7
  235.2 6.7 %all-to-all-done.7 = bf16[2,16,2,1,256]{4,2,0,3,1:T(2,128)(2,1)S(1)} async-done(((bf16[2,16,2,1,256]{4,2,0,3,1:T(2,128)(2,1)}), bf16[2,16,2,1,256]{4,2,0,3,1:T(2,128)(2,1)S(1)}, u32[]{:S(2)}, u32[]{:S(2)}) %all-to-all-start.7) | async-done | bytes 32800 | tf_op jit(solution)/shard_map/all_to_all | solution.py:202
  242.8 3.5 all-to-all-start.8
  247.0 6.6 %all-to-all-done.8 = bf16[2,1,2,16,256]{4,2,0,1,3:T(2,128)(2,1)S(1)} async-done(((bf16[2,1,2,16,256]{4,2,0,1,3:T(2,128)(2,1)}), bf16[2,1,2,16,256]{4,2,0,1,3:T(2,128)(2,1)S(1)}, u32[]{:S(2)}, u32[]{:S(2)}) %all-to-all-start.8) | async-done | bytes 32800 | tf_op jit(solution)/shard_map/all_to_all | solution.py:191
  253.7 2.0 convert_reduce_fusion.10
  268.9 3.5 all-to-all-start.9
  272.4 7.4 %all-to-all-done.9 = bf16[2,16,2,1,256]{4,2,0,3,1:T(2,128)(2,1)S(1)} async-done(((bf16[2,16,2,1,256]{4,2,0,3,1:T(2,128)(2,1)}), bf16[2,16,2,1,256]{4,2,0,3,1:T(2,128)(2,1)S(1)}, u32[]{:S(2)}, u32[]{:S(2)}) %all-to-all-start.9) | async-done | bytes 32800 | tf_op jit(solution)/shard_map/all_to_all | solution.py:202
  280.7 3.5 all-to-all-start.10
  284.2 7.4 %all-to-all-done.10 = bf16[2,1,2,16,256]{4,2,0,1,3:T(2,128)(2,1)S(1)} async-done(((bf16[2,1,2,16,256]{4,2,0,1,3:T(2,128)(2,1)}), bf16[2,1,2,16,256]{4,2,0,1,3:T(2,128)(2,1)S(1)}, u32[]{:S(2)}, u32[]{:S(2)}) %all-to-all-start.10) | async-done | bytes 32800 | tf_op jit(solution)/shard_map/all_to_all | solution.py:191
  305.2 3.7 all-to-all-start.11
  308.9 2.2 convolution_add_fusion.19
  311.0 5.2 %all-to-all-done.11 = bf16[2,16,2,1,256]{4,2,0,3,1:T(2,128)(2,1)S(1)} async-done(((bf16[2,16,2,1,256]{4,2,0,3,1:T(2,128)(2,1)}), bf16[2,16,2,1,256]{4,2,0,3,1:T(2,128)(2,1)S(1)}, u32[]{:S(2)}, u32[]{:S(2)}) %all-to-all-start.11) | async-done | bytes 32800 | tf_op jit(solution)/shard_map/all_to_all | solution.py:202
  317.2 3.5 all-to-all-start.12
  320.8 7.3 %all-to-all-done.12 = bf16[2,1,2,16,256]{4,2,0,1,3:T(2,128)(2,1)S(1)} async-done(((bf16[2,1,2,16,256]{4,2,0,1,3:T(2,128)(2,1)}), bf16[2,1,2,16,256]{4,2,0,1,3:T(2,128)(2,1)S(1)}, u32[]{:S(2)}, u32[]{:S(2)}) %all-to-all-start.12) | async-done | bytes 32800 | tf_op jit(solution)/shard_map/all_to_all | solution.py:191
  339.6 38.5 %psum.79 = f32[2,1024]{1,0:T(2,128)S(1)} all-reduce(f32[2,1024]{1,0:T(2,128)S(1)} %fusion.164), channel_id=1, replica_groups=mesh['tm'=2,'lat'=16] {'tm','lat'}, use_global_device_ids=true, to_apply=%region_88.89 | all-reduce | flops 2048 | bytes 16384 | tf_op jit(solution)/shard_map/psum | solution.py:207
  378.8 90.0 %all-reduce.4.cloned.1.call-done = (f32[256,384]{1,0:T(8,128)}, f32[384,384]{1,0:T(8,128)}, f32[384,256]{1,0:T(8,128)}) async-done(((f32[256,384]{1,0:T(8,128)}, f32[384,384]{1,0:T(8,128)}, f32[384,256]{1,0:T(8,128)}), (f32[256,384]{1,0:T(8,128)}, f32[384,384]{1,0:T(8,128)}, f32[384,256]{1,0:T(8,128)})) %all-reduce.4.cloned.1.call-update) | async-done | bytes 1376272 | tf_op jit(solution)/shard_map/psum | solution.py:207
  (512 shorter events, 108.9 us)
Async XLA Ops:
  9.2 11.4 %copy-start.37 = (f32[256,384]{1,0:T(8,128)S(1)}, f32[256,384]{1,0:T(8,128)}, u32[]{:S(2)}) copy-start(f32[256,384]{1,0:T(8,128)} %param.26) | copy-start | bytes 1179652
  10.6 9.1 %copy-start.91 = (f32[2,1024]{1,0:T(2,128)S(1)}, f32[2,1024]{1,0:T(2,128)}, u32[]{:S(2)}) copy-start(f32[2,1024]{1,0:T(2,128)} %param.29) | copy-start | bytes 24580
  10.8 9.9 %copy-start.39 = (f32[384,256]{1,0:T(8,128)S(1)}, f32[384,256]{1,0:T(8,128)}, u32[]{:S(2)}) copy-start(f32[384,256]{1,0:T(8,128)} %param.28) | copy-start | bytes 1179652
  11.4 15.8 %all-to-all-start = ((bf16[2,1,2,16,256]{4,2,0,1,3:T(2,128)(2,1)}), bf16[2,1,2,16,256]{4,2,0,1,3:T(2,128)(2,1)S(1)}, u32[]{:S(2)}, u32[]{:S(2)}) async-start(bf16[2,1,2,16,256]{4,2,0,1,3:T(2,128)(2,1)} %copy.194), calls=%async_computation | async-start | bytes 65536 | tf_op jit(solution)/shard_map/all_to_all | solution.py:141
  19.8 73.5 %copy-start.139 = (f32[384]{0:T(512)}, f32[384]{0:T(512)S(1)}, u32[]{:S(2)}) copy-start(f32[384]{0:T(512)S(1)} %get-tuple-element.47) | copy-start | bytes 4612
  19.8 76.8 %copy-start.137 = (f32[384]{0:T(512)}, f32[384]{0:T(512)S(1)}, u32[]{:S(2)}) copy-start(f32[384]{0:T(512)S(1)} %get-tuple-element.45) | copy-start | bytes 4612
  20.6 72.7 %copy-start.24 = (bf16[256,384]{1,0:T(8,128)(2,1)}, bf16[256,384]{1,0:T(8,128)(2,1)S(1)}, u32[]{:S(2)}) copy-start(bf16[256,384]{1,0:T(8,128)(2,1)S(1)} %convert_element_type.413) | copy-start | bytes 589828
  21.8 74.9 %copy-start.21 = (bf16[384,384]{1,0:T(8,128)(2,1)}, bf16[384,384]{1,0:T(8,128)(2,1)S(1)}, u32[]{:S(2)}) copy-start(bf16[384,384]{1,0:T(8,128)(2,1)S(1)} %convert_element_type.415) | copy-start | bytes 884740
  28.0 3.0 copy-start.28
  31.0 4.0 copy-start.4
  31.9 3.2 copy-start.93
  60.6 3.0 copy-start.48
  63.7 4.0 copy-start.6
  64.5 3.2 copy-start.95
  93.4 3.1 copy-start.50
  96.5 3.4 copy-start.8
  96.6 3.2 copy-start.109
  96.6 3.2 copy-start.97
  113.0 3.9 copy-start.123
  113.0 19.9 %all-to-all-start.6 = ((bf16[2,1,2,16,256]{4,2,0,1,3:T(2,128)(2,1)}), bf16[2,1,2,16,256]{4,2,0,1,3:T(2,128)(2,1)S(1)}, u32[]{:S(2)}, u32[]{:S(2)}) async-start(bf16[2,1,2,16,256]{4,2,0,1,3:T(2,128)(2,1)} %copy.216), calls=%async_computation.6 | async-start | bytes 65536 | tf_op jit(solution)/shard_map/all_to_all | solution.py:141
  122.7 2.1 copy-start.11
  127.9 2.1 copy-start.13
  133.3 71.8 %copy-start.87 = (f32[1,2,2,128]{3,1,2,0:T(2,128)}, f32[1,2,2,128]{3,1,2,0:T(2,128)S(1)}, u32[]{:S(2)}) copy-start(f32[1,2,2,128]{3,1,2,0:T(2,128)S(1)} %copy.333) | copy-start | bytes 6148
  135.0 70.1 %copy-start.89 = (f32[512]{0:T(512)}, f32[512]{0:T(512)S(1)}, u32[]{:S(2)}) copy-start(f32[512]{0:T(512)S(1)} %rsqrt.155) | copy-start | bytes 6148
  136.3 3.1 copy-start.52
  139.4 4.4 copy-start.2
  139.5 4.2 copy-start.113
  140.6 3.2 copy-start.99
  208.6 5.5 %copy-start.136 = (f32[2,8]{1,0:T(2,128)S(1)}, f32[2,8]{1,0:T(2,128)}, u32[]{:S(2)}) copy-start(f32[2,8]{1,0:T(2,128)} %get-tuple-element.143) | copy-start | bytes 196
  230.8 3.7 copy-start.128
  230.8 11.0 %all-to-all-start.7 = ((bf16[2,16,2,1,256]{4,2,0,3,1:T(2,128)(2,1)}), bf16[2,16,2,1,256]{4,2,0,3,1:T(2,128)(2,1)S(1)}, u32[]{:S(2)}, u32[]{:S(2)}) async-start(bf16[2,16,2,1,256]{4,2,0,3,1:T(2,128)(2,1)} %copy.228), calls=%async_computation.7 | async-start | bytes 65536 | tf_op jit(solution)/shard_map/all_to_all | solution.py:202
  242.8 10.9 %all-to-all-start.8 = ((bf16[2,1,2,16,256]{4,2,0,1,3:T(2,128)(2,1)}), bf16[2,1,2,16,256]{4,2,0,1,3:T(2,128)(2,1)S(1)}, u32[]{:S(2)}, u32[]{:S(2)}) async-start(bf16[2,1,2,16,256]{4,2,0,1,3:T(2,128)(2,1)} %copy.231), calls=%async_computation.8 | async-start | bytes 65536 | tf_op jit(solution)/shard_map/all_to_all | solution.py:191
  265.1 2.2 copy-start.120
  268.0 23.6 %copy-start.36 = (f32[2,1,256,256]{3,2,0,1:T(8,128)S(1)}, f32[2,1,256,256]{3,2,0,1:T(8,128)}, u32[]{:S(2)}) copy-start(f32[2,1,256,256]{3,2,0,1:T(8,128)} %copy.243) | copy-start | bytes 1572868
  268.9 10.9 %all-to-all-start.9 = ((bf16[2,16,2,1,256]{4,2,0,3,1:T(2,128)(2,1)}), bf16[2,16,2,1,256]{4,2,0,3,1:T(2,128)(2,1)S(1)}, u32[]{:S(2)}, u32[]{:S(2)}) async-start(bf16[2,16,2,1,256]{4,2,0,3,1:T(2,128)(2,1)} %copy.238), calls=%async_computation.9 | async-start | bytes 65536 | tf_op jit(solution)/shard_map/all_to_all | solution.py:202
  280.7 10.9 %all-to-all-start.10 = ((bf16[2,1,2,16,256]{4,2,0,1,3:T(2,128)(2,1)}), bf16[2,1,2,16,256]{4,2,0,1,3:T(2,128)(2,1)S(1)}, u32[]{:S(2)}, u32[]{:S(2)}) async-start(bf16[2,1,2,16,256]{4,2,0,1,3:T(2,128)(2,1)} %copy.241), calls=%async_computation.10 | async-start | bytes 65536 | tf_op jit(solution)/shard_map/all_to_all | solution.py:191
  304.3 4.5 copy-start.49
  305.2 11.0 %all-to-all-start.11 = ((bf16[2,16,2,1,256]{4,2,0,3,1:T(2,128)(2,1)}), bf16[2,16,2,1,256]{4,2,0,3,1:T(2,128)(2,1)S(1)}, u32[]{:S(2)}, u32[]{:S(2)}) async-start(bf16[2,16,2,1,256]{4,2,0,3,1:T(2,128)(2,1)} %copy.248), calls=%async_computation.11 | async-start | bytes 65536 | tf_op jit(solution)/shard_map/all_to_all | solution.py:202
  308.9 19.2 %copy-start.35 = (f32[2,1,256,256]{3,2,0,1:T(8,128)S(1)}, f32[2,1,256,256]{3,2,0,1:T(8,128)}, u32[]{:S(2)}) copy-start(f32[2,1,256,256]{3,2,0,1:T(8,128)} %copy.253) | copy-start | bytes 1572868
  317.2 10.9 %all-to-all-start.12 = ((bf16[2,1,2,16,256]{4,2,0,1,3:T(2,128)(2,1)}), bf16[2,1,2,16,256]{4,2,0,1,3:T(2,128)(2,1)S(1)}, u32[]{:S(2)}, u32[]{:S(2)}) async-start(bf16[2,1,2,16,256]{4,2,0,1,3:T(2,128)(2,1)} %copy.251), calls=%async_computation.12 | async-start | bytes 65536 | tf_op jit(solution)/shard_map/all_to_all | solution.py:191
  320.7 148.0 %all-reduce.4.cloned.1.call-start = ((), (), s32[]{:S(2)}) async-start(), calls=%async_computation.13 | async-start | bytes 2752512 | tf_op jit(solution)/shard_map/psum | solution.py:207
  339.2 137.3 %copy-start.72 = (f32[256,384]{1,0:T(8,128)S(1)}, f32[256,384]{1,0:T(8,128)}, u32[]{:S(2)}) copy-start(f32[256,384]{1,0:T(8,128)} %param.30) | copy-start | bytes 1179652
  468.7 7.7 %copy-start.71 = (f32[256,384]{1,0:T(8,128)S(1)}, f32[256,384]{1,0:T(8,128)}, u32[]{:S(2)}) copy-start(f32[256,384]{1,0:T(8,128)} %param.34) | copy-start | bytes 1179652
  470.5 6.0 %copy-start.38 = (f32[256,384]{1,0:T(8,128)S(1)}, f32[256,384]{1,0:T(8,128)}, u32[]{:S(2)}) copy-start(f32[256,384]{1,0:T(8,128)} %param.26) | copy-start | bytes 1179652
  472.4 3.4 copy-start.129
  472.4 3.4 copy-start.130
  473.1 2.7 copy-start.92
  478.3 2.1 copy-start.70
  (104 other events, 121.1 us)
Sparse Core Ops, SparseCore 0:
  339.3 129.3 all-reduce.3
where the time goes:
time: 499 us; the launch traced here: 491 us
  waiting for transfers between devices  136 us (27%)
  blocking collectives  134 us (27%)
  matrix products  61.3 us (12%)
  local copies, waits for them, and re-layouts  61.2 us (12%)
  other arithmetic  44.3 us (9%)
  starting transfers between devices  33.5 us (7%)
  between operations  20.2 us (4%)
    psum x1, waiting for transfers between devices, per_device(): grads = lax.psum(totals, ('tm', 'lat'))  90 us
    psum x1, blocking collectives, per_device(): num_total, den_total = lax.psum((num_part, den_part), 'lat')  42.5 us
    psum x1, blocking collectives, per_device(): grads = lax.psum(totals, ('tm', 'lat'))  38.5 us
    dot_general x12, matrix products, corrector_forward(): jnp.dot(h_low, weights[k], preferred_element_type=jnp.float32)  31.7 us
    all_to_all x3, blocking collectives, per_device(): lax.all_to_all(coeff, 'lat', split_axis=1, concat_axis=3, tiled=True)  29.9 us
    unnamed x297, local copies, waits for them, and re-layouts  29.6 us
    all_to_all x3, waiting for transfers between devices, per_device(): lax.all_to_all(back_coeff, 'lat', split_axis=3, concat_axis=1, tiled=True)  21.3 us
    all_to_all x2, blocking collectives, to_grid(): lax.all_to_all(sums, 'lat', split_axis=3, concat_axis=1, tiled=True)  20.1 us
  transfers between devices with their start and end apart: 9, of which 8 were waited for; matrix products, arithmetic and copies ran while one was open for 4% of the time, Pallas kernels for 0%

commit v1 on v0

--- a/solution.py
+++ b/solution.py
@@ -138,7 +138,13 @@
             "mnr,tmpnc->tmprc", plg, state.astype(jnp.bfloat16), preferred_element_type=jnp.float32
         ).astype(jnp.bfloat16)
         return fourier_sum(
-            finv, lax.all_to_all(sums, "lat", split_axis=3, concat_axis=1, tiled=True)
+            finv,
+            jnp.concatenate(
+                lax.all_to_all(
+                    jnp.stack(jnp.split(sums, lax.axis_size("lat"), axis=3)), "lat", 0, 0
+                ),
+                axis=1,
+            ),
         )
 
     def column_pass(grid):

time: 499 us -> 517 us (1.036)
  local copies, waits for them, and re-layouts: 61.2 us -> 80.3 us
    unnamed x297 -> x383, local copies, waits for them, and re-layouts: 29.6 us -> 50.5 us
where the time goes in v1:
time: 517 us; the launch traced here: 508 us
  blocking collectives  135 us (26%)
  waiting for transfers between devices  131 us (25%)
  local copies, waits for them, and re-layouts  80.3 us (16%)
  matrix products  60.9 us (12%)
  other arithmetic  47.8 us (9%)
  starting transfers between devices  33.2 us (6%)
  between operations  20.4 us (4%)
    psum x1, waiting for transfers between devices, per_device(): grads = lax.psum(totals, ('tm', 'lat'))  88.4 us
    unnamed x383, local copies, waits for them, and re-layouts  50.5 us
    psum x1, blocking collectives, per_device(): num_total, den_total = lax.psum((num_part, den_part), 'lat')  42.5 us
    psum x1, blocking collectives, per_device(): grads = lax.psum(totals, ('tm', 'lat'))  38.6 us
    dot_general x12, matrix products, corrector_forward(): jnp.dot(h_low, weights[k], preferred_element_type=jnp.float32)  31.7 us
    all_to_all x3, blocking collectives, per_device(): lax.all_to_all(coeff, 'lat', split_axis=1, concat_axis=3, tiled=True)  30.1 us
    all_to_all x2, blocking collectives, to_grid(): lax.all_to_all(jnp.stack(jnp.split(sums, lax.axis_size('lat'), axis=3)),...  20.1 us
    all_to_all x3, waiting for transfers between devices, per_device(): lax.all_to_all(back_sums, 'lat', split_axis=1, concat_axis=3, tiled=True)  18.8 us
  transfers between devices with their start and end apart: 9, of which 8 were waited for; matrix products, arithmetic and copies ran while one was open for 4% of the time, Pallas kernels for 0%

profile of v1, /device:TPU:0, one launch (start us, length us, event | category | flops | bytes accessed | tf_op | source)
XLA Modules:
  0.0 508.5 jit_solution(5362676561432040328)
XLA Ops:
  20.1 8.3 %all-to-all-start = ((bf16[16,2,1,2,1,256]{5,3,1,4,2,0:T(2,128)(2,1)}), bf16[16,2,1,2,1,256]{5,3,1,4,2,0:T(2,128)(2,1)S(1)}, u32[]{:S(2)}, u32[]{:S(2)}) async-start(bf16[16,2,1,2,1,256]{5,3,1,4,2,0:T(2,128)(2,1)} %constant_dynamic-update-slice_fusion), calls=%async_computation | async-start | bytes 65536 | tf_op jit(solution)/shard_map/all_to_all | solution.py:143
  30.6 5.3 %all-to-all-done = bf16[16,2,1,2,1,256]{5,3,1,4,2,0:T(2,128)(2,1)S(1)} async-done(((bf16[16,2,1,2,1,256]{5,3,1,4,2,0:T(2,128)(2,1)}), bf16[16,2,1,2,1,256]{5,3,1,4,2,0:T(2,128)(2,1)S(1)}, u32[]{:S(2)}, u32[]{:S(2)}) %all-to-all-start) | async-done | bytes 32800 | tf_op jit(solution)/shard_map/all_to_all | solution.py:143
  36.7 3.0 fusion.214
  40.6 3.2 fusion.212
  47.1 10.0 %all_to_all.159 = bf16[2,16,2,1,256]{4,2,0,3,1:T(2,128)(2,1)S(1)} all-to-all(bf16[2,16,2,1,256]{4,2,0,3,1:T(2,128)(2,1)S(1)} %copy.1491), channel_id=1, replica_groups=mesh['tm'=2,'lat'=16] {'lat'}, dimensions={1} | all-to-all | bytes 65536 | tf_op jit(solution)/shard_map/all_to_all | solution.py:175
  57.7 10.1 %all_to_all.160 = bf16[16,2,1,2,1,256]{5,3,1,4,2,0:T(2,128)(2,1)S(1)} all-to-all(bf16[16,2,1,2,1,256]{5,3,1,4,2,0:T(2,128)(2,1)S(1)} %constant_dynamic-update-slice_fusion.16), channel_id=1, replica_groups=mesh['tm'=2,'lat'=16] {'lat'}, dimensions={0} | all-to-all | bytes 65536 | tf_op jit(solution)/shard_map/all_to_all | solution.py:143
  70.2 3.0 fusion.210
  74.0 3.2 fusion.208
  77.9 1.9 broadcast_multiply_fusion.1
  80.0 10.0 %all_to_all.161 = bf16[2,16,2,1,256]{4,2,0,3,1:T(2,128)(2,1)S(1)} all-to-all(bf16[2,16,2,1,256]{4,2,0,3,1:T(2,128)(2,1)S(1)} %copy.1498), channel_id=1, replica_groups=mesh['tm'=2,'lat'=16] {'lat'}, dimensions={1} | all-to-all | bytes 65536 | tf_op jit(solution)/shard_map/all_to_all | solution.py:175
  90.6 10.0 %all_to_all.162 = bf16[16,2,1,2,1,256]{5,3,1,4,2,0:T(2,128)(2,1)S(1)} all-to-all(bf16[16,2,1,2,1,256]{5,3,1,4,2,0:T(2,128)(2,1)S(1)} %constant_dynamic-update-slice_fusion.32), channel_id=1, replica_groups=mesh['tm'=2,'lat'=16] {'lat'}, dimensions={0} | all-to-all | bytes 65536 | tf_op jit(solution)/shard_map/all_to_all | solution.py:143
  103.6 3.1 fusion.206
  107.5 3.2 fusion.204
  110.9 1.9 broadcast_multiply_fusion
  113.0 10.2 %all_to_all.163 = bf16[2,16,2,1,256]{4,2,0,3,1:T(2,128)(2,1)S(1)} all-to-all(bf16[2,16,2,1,256]{4,2,0,3,1:T(2,128)(2,1)S(1)} %copy.1504), channel_id=1, replica_groups=mesh['tm'=2,'lat'=16] {'lat'}, dimensions={1} | all-to-all | bytes 65536 | tf_op jit(solution)/shard_map/all_to_all | solution.py:175
  132.8 3.6 all-to-all-start.6
  137.3 2.0 copy.1490
  139.3 1.9 add.540
  142.3 2.1 copy.1497
  144.4 1.9 add.549
  147.4 2.1 copy.1503
  149.5 1.9 add.558
  155.8 3.1 fusion.202
  160.1 3.2 fusion.200
  164.7 2.1 copy.1509
  166.7 2.1 add.567
  170.0 42.5 %all-reduce.1 = (f32[1,2,8]{2,1,0:T(2,128)S(1)}, f32[1,2,8]{2,1,0:T(2,128)S(1)}, f32[1,2,8]{2,1,0:T(2,128)S(1)}, f32[1,2,8]{2,1,0:T(2,128)S(1)}, f32[2,8]{1,0:T(2,128)S(1)}) all-reduce(f32[1,2,8]{2,1,0:T(2,128)S(1)} %bitcast.793, f32[1,2,8]{2,1,0:T(2,128)S(1)} %bitcast.794, ...), channel_id=1, replica_groups=mesh['tm'=2,'lat'=16] {'lat'}, use_global_device_ids=true, to_apply=%region_31.32 | all-reduce | flops 80 | bytes 640 | tf_op jit(solution)/shard_map/psum | solution.py:169
  226.2 2.2 fusion.224
  228.3 3.4 psum.75
  233.5 2.0 copy.1523
  236.3 2.0 copy.1543
  239.2 2.0 copy.1533
  245.8 3.5 all-to-all-start.7
  250.0 6.7 %all-to-all-done.7 = bf16[2,16,2,1,256]{4,2,0,3,1:T(2,128)(2,1)S(1)} async-done(((bf16[2,16,2,1,256]{4,2,0,3,1:T(2,128)(2,1)}), bf16[2,16,2,1,256]{4,2,0,3,1:T(2,128)(2,1)S(1)}, u32[]{:S(2)}, u32[]{:S(2)}) %all-to-all-start.7) | async-done | bytes 32800 | tf_op jit(solution)/shard_map/all_to_all | solution.py:208
  257.7 3.5 all-to-all-start.8
  262.5 6.1 %all-to-all-done.8 = bf16[2,1,2,16,256]{4,2,0,1,3:T(2,128)(2,1)S(1)} async-done(((bf16[2,1,2,16,256]{4,2,0,1,3:T(2,128)(2,1)}), bf16[2,1,2,16,256]{4,2,0,1,3:T(2,128)(2,1)S(1)}, u32[]{:S(2)}, u32[]{:S(2)}) %all-to-all-start.8) | async-done | bytes 32800 | tf_op jit(solution)/shard_map/all_to_all | solution.py:197
  283.7 3.5 all-to-all-start.9
  287.9 6.8 %all-to-all-done.9 = bf16[2,16,2,1,256]{4,2,0,3,1:T(2,128)(2,1)S(1)} async-done(((bf16[2,16,2,1,256]{4,2,0,3,1:T(2,128)(2,1)}), bf16[2,16,2,1,256]{4,2,0,3,1:T(2,128)(2,1)S(1)}, u32[]{:S(2)}, u32[]{:S(2)}) %all-to-all-start.9) | async-done | bytes 32800 | tf_op jit(solution)/shard_map/all_to_all | solution.py:208
  295.6 3.5 all-to-all-start.10
  300.4 6.1 %all-to-all-done.10 = bf16[2,1,2,16,256]{4,2,0,1,3:T(2,128)(2,1)S(1)} async-done(((bf16[2,1,2,16,256]{4,2,0,1,3:T(2,128)(2,1)}), bf16[2,1,2,16,256]{4,2,0,1,3:T(2,128)(2,1)S(1)}, u32[]{:S(2)}, u32[]{:S(2)}) %all-to-all-start.10) | async-done | bytes 32800 | tf_op jit(solution)/shard_map/all_to_all | solution.py:197
  322.2 3.7 all-to-all-start.11
  325.9 2.1 convolution_add_fusion.19
  328.0 5.2 %all-to-all-done.11 = bf16[2,16,2,1,256]{4,2,0,3,1:T(2,128)(2,1)S(1)} async-done(((bf16[2,16,2,1,256]{4,2,0,3,1:T(2,128)(2,1)}), bf16[2,16,2,1,256]{4,2,0,3,1:T(2,128)(2,1)S(1)}, u32[]{:S(2)}, u32[]{:S(2)}) %all-to-all-start.11) | async-done | bytes 32800 | tf_op jit(solution)/shard_map/all_to_all | solution.py:208
  334.2 3.5 all-to-all-start.12
  338.5 6.6 %all-to-all-done.12 = bf16[2,1,2,16,256]{4,2,0,1,3:T(2,128)(2,1)S(1)} async-done(((bf16[2,1,2,16,256]{4,2,0,1,3:T(2,128)(2,1)}), bf16[2,1,2,16,256]{4,2,0,1,3:T(2,128)(2,1)S(1)}, u32[]{:S(2)}, u32[]{:S(2)}) %all-to-all-start.12) | async-done | bytes 32800 | tf_op jit(solution)/shard_map/all_to_all | solution.py:197
  358.8 38.6 %psum.79 = f32[2,1024]{1,0:T(2,128)S(1)} all-reduce(f32[2,1024]{1,0:T(2,128)S(1)} %fusion.164), channel_id=1, replica_groups=mesh['tm'=2,'lat'=16] {'tm','lat'}, use_global_device_ids=true, to_apply=%region_88.89 | all-reduce | flops 2048 | bytes 16384 | tf_op jit(solution)/shard_map/psum | solution.py:213
  397.9 88.4 %all-reduce.4.cloned.1.call-done = (f32[256,384]{1,0:T(8,128)}, f32[384,384]{1,0:T(8,128)}, f32[384,256]{1,0:T(8,128)}) async-done(((f32[256,384]{1,0:T(8,128)}, f32[384,384]{1,0:T(8,128)}, f32[384,256]{1,0:T(8,128)}), (f32[256,384]{1,0:T(8,128)}, f32[384,384]{1,0:T(8,128)}, f32[384,256]{1,0:T(8,128)})) %all-reduce.4.cloned.1.call-update) | async-done | bytes 1376272 | tf_op jit(solution)/shard_map/psum | solution.py:213
  488.1 1.9 multiply_reduce_fusion.24
  (602 shorter events, 132.1 us)
Async XLA Ops:
  9.8 19.4 %copy-start.39 = (f32[256,384]{1,0:T(8,128)S(1)}, f32[256,384]{1,0:T(8,128)}, u32[]{:S(2)}) copy-start(f32[256,384]{1,0:T(8,128)} %param.26) | copy-start | bytes 1179652
  14.3 14.2 %copy-start.102 = (f32[2,1024]{1,0:T(2,128)S(1)}, f32[2,1024]{1,0:T(2,128)}, u32[]{:S(2)}) copy-start(f32[2,1024]{1,0:T(2,128)} %param.29) | copy-start | bytes 24580
  14.9 14.4 %copy-start.41 = (f32[384,256]{1,0:T(8,128)S(1)}, f32[384,256]{1,0:T(8,128)}, u32[]{:S(2)}) copy-start(f32[384,256]{1,0:T(8,128)} %param.28) | copy-start | bytes 1179652
  20.1 15.8 %all-to-all-start = ((bf16[16,2,1,2,1,256]{5,3,1,4,2,0:T(2,128)(2,1)}), bf16[16,2,1,2,1,256]{5,3,1,4,2,0:T(2,128)(2,1)S(1)}, u32[]{:S(2)}, u32[]{:S(2)}) async-start(bf16[16,2,1,2,1,256]{5,3,1,4,2,0:T(2,128)(2,1)} %constant_dynamic-update-slice_fusion), calls=%async_computation | async-start | bytes 65536 | tf_op jit(solution)/shard_map/all_to_all | solution.py:143
  28.5 41.3 %copy-start.151 = (f32[384]{0:T(512)}, f32[384]{0:T(512)S(1)}, u32[]{:S(2)}) copy-start(f32[384]{0:T(512)S(1)} %get-tuple-element.47) | copy-start | bytes 4612
  28.5 44.8 %copy-start.149 = (f32[384]{0:T(512)}, f32[384]{0:T(512)S(1)}, u32[]{:S(2)}) copy-start(f32[384]{0:T(512)S(1)} %get-tuple-element.45) | copy-start | bytes 4612
  29.3 73.8 %copy-start.24 = (bf16[256,384]{1,0:T(8,128)(2,1)}, bf16[256,384]{1,0:T(8,128)(2,1)S(1)}, u32[]{:S(2)}) copy-start(bf16[256,384]{1,0:T(8,128)(2,1)S(1)} %convert_element_type.413) | copy-start | bytes 589828
  30.5 76.4 %copy-start.21 = (bf16[384,384]{1,0:T(8,128)(2,1)}, bf16[384,384]{1,0:T(8,128)(2,1)S(1)}, u32[]{:S(2)}) copy-start(bf16[384,384]{1,0:T(8,128)(2,1)S(1)} %convert_element_type.415) | copy-start | bytes 884740
  36.7 3.0 copy-start.28
  39.7 4.0 copy-start.4
  40.6 3.2 copy-start.104
  70.2 3.0 copy-start.51
  73.2 4.0 copy-start.6
  74.0 3.2 copy-start.106
  103.6 3.1 copy-start.52
  106.7 4.0 copy-start.8
  106.8 3.9 copy-start.118
  107.5 3.2 copy-start.108
  132.8 3.6 copy-start.132
  132.8 19.7 %all-to-all-start.6 = ((bf16[16,2,1,2,1,256]{5,3,1,4,2,0:T(2,128)(2,1)}), bf16[16,2,1,2,1,256]{5,3,1,4,2,0:T(2,128)(2,1)S(1)}, u32[]{:S(2)}, u32[]{:S(2)}) async-start(bf16[16,2,1,2,1,256]{5,3,1,4,2,0:T(2,128)(2,1)} %constant_dynamic-update-slice_fusion.48), calls=%async_computation.6 | async-start | bytes 65536 | tf_op jit(solution)/shard_map/all_to_all | solution.py:143
  142.3 2.1 copy-start.11
  147.4 2.1 copy-start.13
  155.8 3.1 copy-start.54
  158.9 4.4 copy-start.2
  243.9 5.5 %copy-start.135 = (f32[384]{0:T(512)S(1)}, f32[384]{0:T(512)}, u32[]{:S(2)}) copy-start(f32[384]{0:T(512)} %get-tuple-element.86) | copy-start | bytes 4612
  243.9 5.5 %copy-start.139 = (f32[384]{0:T(512)S(1)}, f32[384]{0:T(512)}, u32[]{:S(2)}) copy-start(f32[384]{0:T(512)} %get-tuple-element.84) | copy-start | bytes 4612
  245.0 23.6 %copy-start.38 = (f32[2,1,256,256]{3,2,0,1:T(8,128)S(1)}, f32[2,1,256,256]{3,2,0,1:T(8,128)}, u32[]{:S(2)}) copy-start(f32[2,1,256,256]{3,2,0,1:T(8,128)} %copy.1523) | copy-start | bytes 1572868
  245.8 10.9 %all-to-all-start.7 = ((bf16[2,16,2,1,256]{4,2,0,3,1:T(2,128)(2,1)}), bf16[2,16,2,1,256]{4,2,0,3,1:T(2,128)(2,1)S(1)}, u32[]{:S(2)}, u32[]{:S(2)}) async-start(bf16[2,16,2,1,256]{4,2,0,3,1:T(2,128)(2,1)} %copy.1518), calls=%async_computation.7 | async-start | bytes 65536 | tf_op jit(solution)/shard_map/all_to_all | solution.py:208
  257.7 10.9 %all-to-all-start.8 = ((bf16[2,1,2,16,256]{4,2,0,1,3:T(2,128)(2,1)}), bf16[2,1,2,16,256]{4,2,0,1,3:T(2,128)(2,1)S(1)}, u32[]{:S(2)}, u32[]{:S(2)}) async-start(bf16[2,1,2,16,256]{4,2,0,1,3:T(2,128)(2,1)} %copy.1521), calls=%async_computation.8 | async-start | bytes 65536 | tf_op jit(solution)/shard_map/all_to_all | solution.py:197
  279.4 2.2 copy-start.125
  282.8 4.4 copy-start.145
  282.9 23.6 %copy-start.37 = (f32[2,1,256,256]{3,2,0,1:T(8,128)S(1)}, f32[2,1,256,256]{3,2,0,1:T(8,128)}, u32[]{:S(2)}) copy-start(f32[2,1,256,256]{3,2,0,1:T(8,128)} %copy.1533) | copy-start | bytes 1572868
  283.7 10.9 %all-to-all-start.9 = ((bf16[2,16,2,1,256]{4,2,0,3,1:T(2,128)(2,1)}), bf16[2,16,2,1,256]{4,2,0,3,1:T(2,128)(2,1)S(1)}, u32[]{:S(2)}, u32[]{:S(2)}) async-start(bf16[2,16,2,1,256]{4,2,0,3,1:T(2,128)(2,1)} %copy.1528), calls=%async_computation.9 | async-start | bytes 65536 | tf_op jit(solution)/shard_map/all_to_all | solution.py:208
  295.6 10.9 %all-to-all-start.10 = ((bf16[2,1,2,16,256]{4,2,0,1,3:T(2,128)(2,1)}), bf16[2,1,2,16,256]{4,2,0,1,3:T(2,128)(2,1)S(1)}, u32[]{:S(2)}, u32[]{:S(2)}) async-start(bf16[2,1,2,16,256]{4,2,0,1,3:T(2,128)(2,1)} %copy.1531), calls=%async_computation.10 | async-start | bytes 65536 | tf_op jit(solution)/shard_map/all_to_all | solution.py:197
  316.5 2.2 copy-start.123
  321.4 4.5 copy-start.46
  322.2 11.0 %all-to-all-start.11 = ((bf16[2,16,2,1,256]{4,2,0,3,1:T(2,128)(2,1)}), bf16[2,16,2,1,256]{4,2,0,3,1:T(2,128)(2,1)S(1)}, u32[]{:S(2)}, u32[]{:S(2)}) async-start(bf16[2,16,2,1,256]{4,2,0,3,1:T(2,128)(2,1)} %copy.1538), calls=%async_computation.11 | async-start | bytes 65536 | tf_op jit(solution)/shard_map/all_to_all | solution.py:208
  325.9 19.2 %copy-start.36 = (f32[2,1,256,256]{3,2,0,1:T(8,128)S(1)}, f32[2,1,256,256]{3,2,0,1:T(8,128)}, u32[]{:S(2)}) copy-start(f32[2,1,256,256]{3,2,0,1:T(8,128)} %copy.1543) | copy-start | bytes 1572868
  334.2 10.9 %all-to-all-start.12 = ((bf16[2,1,2,16,256]{4,2,0,1,3:T(2,128)(2,1)}), bf16[2,1,2,16,256]{4,2,0,1,3:T(2,128)(2,1)S(1)}, u32[]{:S(2)}, u32[]{:S(2)}) async-start(bf16[2,1,2,16,256]{4,2,0,1,3:T(2,128)(2,1)} %copy.1541), calls=%async_computation.12 | async-start | bytes 65536 | tf_op jit(solution)/shard_map/all_to_all | solution.py:197
  337.7 148.6 %all-reduce.4.cloned.1.call-start = ((), (), s32[]{:S(2)}) async-start(), calls=%async_computation.13 | async-start | bytes 2752512 | tf_op jit(solution)/shard_map/psum | solution.py:213
  346.7 2.1 copy-start.113
  357.6 136.5 %copy-start.74 = (f32[256,384]{1,0:T(8,128)S(1)}, f32[256,384]{1,0:T(8,128)}, u32[]{:S(2)}) copy-start(f32[256,384]{1,0:T(8,128)} %param.30) | copy-start | bytes 1179652
  486.4 7.7 %copy-start.73 = (f32[256,384]{1,0:T(8,128)S(1)}, f32[256,384]{1,0:T(8,128)}, u32[]{:S(2)}) copy-start(f32[256,384]{1,0:T(8,128)} %param.34) | copy-start | bytes 1179652
  488.1 6.0 %copy-start.40 = (f32[256,384]{1,0:T(8,128)S(1)}, f32[256,384]{1,0:T(8,128)}, u32[]{:S(2)}) copy-start(f32[256,384]{1,0:T(8,128)} %param.26) | copy-start | bytes 1179652
  490.0 3.4 copy-start.141
  490.0 3.4 copy-start.142
  490.7 2.7 copy-start.103
  496.0 2.1 copy-start.72
  (117 other events, 126.2 us)
Sparse Core Ops, SparseCore 0:
  357.0 129.3 all-reduce.3
